TPU v7x, 256 devices: a whole 4x4x8 slice. The times are simulated.
256 devices in a mesh: seq: 32 (over x, z), head: 8 (over y, core).
Axes of the slice: x: 4, y: 4, z: 8, core: 2. Of those that a mesh axis runs over, the one named last changes fastest.
Arguments:
- tokens: bfloat16 [32768, 3072], P(('seq', 'head')), may hold values from -150 to 150
- norm_gain: float32 [3072], replicated, may hold values from 0.1 to 1.9
- w_query: bfloat16 [3072, 3072], P(None, 'head'), may hold values from -0.15625 to 0.15625
- w_key: bfloat16 [3072, 1024], P(None, 'head'), may hold values from -0.15625 to 0.15625
- w_value: bfloat16 [3072, 1024], P(None, 'head'), may hold values from -0.109375 to 0.109375
- w_out: bfloat16 [3072, 3072], P('head'), may hold values from -1.5 to 1.5
- long_cache: bfloat16 [2, 32768, 1024], P(None, 'seq', 'head'), may hold values from -244 to 244
- short_cache: bfloat16 [2, 8192, 1024], P(None, 'seq', 'head'), may hold values from -244 to 244
- slot_owner: int32 [8192], P('seq'), may hold values from -1 to 63, as said below
- new_len: int32 [64], replicated, may hold values from 2 to 1024, as said below
- cache_len: int32 [64], replicated, may hold values from 32 to 85, as said below
Outputs:
- layer_out: bfloat16 [32768, 3072], P(('seq', 'head'))
Inputs may be any that keep to these rules, and one draw needn't show every extreme that they name: `new_len`: lengths in order after the lead request's 64 tokens; they sum to 32704, and one request has exactly 1024 new tokens. `cache_len`: equals the number of short-cache slots that the request owns; one request has exactly 85. `slot_owner`: A request's slots are contiguous and lie in the block of 256 slots whose index equals that of the block of 1024 tokens holding the request's first new token.
All inputs are finite; a program needn't handle non-finite values.
Results may differ from a plain program's by a relative error of at most 0.02.
The roundings to bfloat16 on the way count: a program that leaves them out, or rounds other values in their place, can miss the bound.
Values may be sent and summed in bfloat16 or wider, within the bound.
A program may use at most 128 MiB of HBM per device.

v0:
```python
import math
import jax
import jax.numpy as jnp
from jax import lax
from jax.sharding import PartitionSpec as P

HD = 128
LEAD = 64
THETA_LOG = math.log(500000.0)


def from_behind(block, axis, distance):
    devices = range(lax.axis_size(axis))
    route = [(i - distance, i) for i in devices if i - distance in devices]
    return lax.ppermute(block, axis, route)


def rotate(field, position):
    half = field.shape[-1] // 2
    frequency = jnp.exp(jnp.arange(half, dtype=jnp.float32) * (-2.0 * THETA_LOG / field.shape[-1]))
    angle = position.astype(jnp.float32)[:, None] * frequency[None, :]
    cosine = jnp.cos(angle)[:, None, :]
    sine_part = jnp.sin(angle)[:, None, :]
    first_half = field[..., :half]
    second_half = field[..., half:]
    return jnp.concatenate(
        [
            first_half * cosine - second_half * sine_part,
            second_half * cosine + first_half * sine_part,
        ],
        axis=-1,
    )


def request_starts(new_len):
    return LEAD + jnp.cumsum(new_len) - new_len


def request_of(position_index, starts):
    passed = (starts[None, :] <= position_index[:, None]).astype(jnp.int32)
    request = jnp.sum(passed, axis=1) - 1
    return jnp.where(request < 0, starts.shape[0], request)


def position_of(position_index, request, starts, cache_len, long_len):
    number = starts.shape[0]
    select = jnp.arange(number, dtype=jnp.int32)[None, :] == request[:, None]
    begin = jnp.sum(jnp.where(select, starts[None, :], 0), axis=1)
    cached = jnp.sum(jnp.where(select, cache_len[None, :], 0), axis=1)
    return jnp.where(request == number, position_index + long_len, position_index - begin + cached)


def normalize(tokens, norm_gain):
    values = tokens.astype(jnp.float32)
    mean_square = jnp.mean(values * values, axis=-1, keepdims=True)
    return (values * lax.rsqrt(mean_square + 1e-05) * norm_gain).astype(jnp.bfloat16)


def raw_scores(queries, keys):
    return jnp.einsum("bgph,ngh->bgpn", queries, keys, preferred_element_type=jnp.float32) * (
        1.0 / math.sqrt(keys.shape[-1])
    )


def finish_state(scores, values):
    highest = jnp.max(scores, axis=-1)
    weights = jnp.exp(scores - highest[..., None])
    summed = jnp.sum(weights, axis=-1)
    mixture = jnp.einsum(
        "bgpn,ngh->bgph", weights.astype(jnp.bfloat16), values, preferred_element_type=jnp.float32
    )
    return (highest, summed, mixture)


def masked_state(queries, keys, values, valid):
    scores = jnp.where(valid[:, None, None, :], raw_scores(queries, keys), -jnp.inf)
    return finish_state(scores, values)


def plain_state(queries, keys, values):
    return finish_state(raw_scores(queries, keys), values)


def combine(former, latter):
    highest = jnp.maximum(former[0], latter[0])
    scale_former = jnp.exp(former[0] - highest)
    scale_latter = jnp.exp(latter[0] - highest)
    summed = former[1] * scale_former + latter[1] * scale_latter
    mixture = former[2] * scale_former[..., None] + latter[2] * scale_latter[..., None]
    return (highest, summed, mixture)


def on_device(
    tokens,
    norm_gain,
    w_query,
    w_key,
    w_value,
    w_out,
    long_cache,
    short_cache,
    slot_owner,
    new_len,
    cache_len,
):
    seq_index = lax.axis_index("seq")
    long_len = long_cache.shape[1] * lax.axis_size("seq")
    kv_heads = w_key.shape[1] // HD
    q_heads = w_query.shape[1] // HD
    per_kv = q_heads // kv_heads
    slots = short_cache.shape[1]
    q_width = w_query.shape[1]
    k_width = w_key.shape[1]
    earlier_slots, earlier_owner = from_behind((short_cache, slot_owner), "seq", 1)
    normed = normalize(tokens, norm_gain)
    piece = lax.all_gather(normed, "head", axis=0, tiled=True)
    projected = jnp.concatenate(
        [
            jnp.dot(piece, w_query, preferred_element_type=jnp.float32),
            jnp.dot(piece, w_key, preferred_element_type=jnp.float32),
            jnp.dot(piece, w_value, preferred_element_type=jnp.float32),
        ],
        axis=1,
    )
    local_rows = projected.shape[0]
    starts = request_starts(new_len)
    token_index = seq_index * local_rows + jnp.arange(local_rows, dtype=jnp.int32)
    request = request_of(token_index, starts)
    position = position_of(token_index, request, starts, cache_len, long_len)
    before_index = token_index - local_rows
    before_request = request_of(before_index, starts)
    queries = rotate(projected[:, :q_width].reshape(local_rows, q_heads, HD), position).astype(
        jnp.bfloat16
    )
    queries = queries.reshape(local_rows, kv_heads, per_kv, HD)
    keys = rotate(
        projected[:, q_width : q_width + k_width].reshape(local_rows, kv_heads, HD), position
    ).astype(jnp.bfloat16)
    values = projected[:, q_width + k_width :].astype(jnp.bfloat16)
    fresh = jnp.stack([keys.reshape(local_rows, k_width), values])
    earlier_fresh = from_behind(fresh, "seq", 1)
    has_before = seq_index > 0
    new_rows = jnp.concatenate([earlier_fresh, fresh], axis=1)
    new_keys = new_rows[0].reshape(-1, kv_heads, HD)
    new_values = new_rows[1].reshape(-1, kv_heads, HD)
    slot_rows = jnp.concatenate([earlier_slots, short_cache], axis=1)
    slot_keys = slot_rows[0].reshape(-1, kv_heads, HD)
    slot_values = slot_rows[1].reshape(-1, kv_heads, HD)
    new_request = jnp.concatenate([jnp.where(has_before, before_request, -1), request])
    new_index = jnp.concatenate([before_index, token_index])
    slot_request = jnp.concatenate([jnp.where(has_before, earlier_owner, -1), slot_owner]).astype(
        jnp.int32
    )
    slot_index = jnp.full((2 * slots,), -1, jnp.int32)
    block_rows = min(local_rows, 512)
    block_count = local_rows // block_rows
    window = local_rows + block_rows

    def local_block(item):
        block_queries, block_request, block_index, block_number = item
        begin = block_number * block_rows
        window_keys = jnp.concatenate(
            [lax.dynamic_slice_in_dim(new_keys, begin, window, 0), slot_keys], axis=0
        )
        window_values = jnp.concatenate(
            [lax.dynamic_slice_in_dim(new_values, begin, window, 0), slot_values], axis=0
        )
        window_request = jnp.concatenate(
            [lax.dynamic_slice_in_dim(new_request, begin, window, 0), slot_request]
        )
        window_index = jnp.concatenate(
            [lax.dynamic_slice_in_dim(new_index, begin, window, 0), slot_index]
        )
        valid = (window_request[None, :] == block_request[:, None]) & (
            window_index[None, :] <= block_index[:, None]
        )
        return masked_state(block_queries, window_keys, window_values, valid)

    highest, summed, mixture = lax.map(
        local_block,
        (
            queries.reshape(block_count, block_rows, kv_heads, per_kv, HD),
            request.reshape(block_count, block_rows),
            token_index.reshape(block_count, block_rows),
            jnp.arange(block_count, dtype=jnp.int32),
        ),
    )
    highest = highest.reshape(local_rows, kv_heads, per_kv)
    summed = summed.reshape(local_rows, kv_heads, per_kv)
    mixture = mixture.reshape(local_rows, kv_heads, per_kv, HD)
    lead_queries = queries[:LEAD]
    start_state = (
        jnp.full((LEAD, kv_heads, per_kv), -1e30, jnp.float32),
        jnp.zeros((LEAD, kv_heads, per_kv), jnp.float32),
        jnp.zeros((LEAD, kv_heads, per_kv, HD), jnp.float32),
    )
    piece = lax.all_gather(long_cache, "seq", axis=1, tiled=True)
    long_state = combine(
        start_state,
        plain_state(
            lead_queries, piece[0].reshape(-1, kv_heads, HD), piece[1].reshape(-1, kv_heads, HD)
        ),
    )
    long_highest = jnp.where(seq_index == 0, long_state[0], -1e30)
    joined = combine(
        (highest[:LEAD], summed[:LEAD], mixture[:LEAD]),
        (long_highest, long_state[1], long_state[2]),
    )
    summed = jnp.concatenate([joined[1], summed[LEAD:]], axis=0)
    mixture = jnp.concatenate([joined[2], mixture[LEAD:]], axis=0)
    attended = (mixture / summed[..., None]).astype(jnp.bfloat16).reshape(local_rows, q_width)
    gathered_sum = lax.psum_scatter(
        jnp.dot(attended, w_out, preferred_element_type=jnp.float32).astype(jnp.bfloat16),
        "head",
        scatter_dimension=0,
        tiled=True,
    )
    return gathered_sum


def solution(mesh):
    placed = (
        P(("seq", "head"), None),
        P(),
        P(None, "head"),
        P(None, "head"),
        P(None, "head"),
        P("head", None),
        P(None, "seq", "head"),
        P(None, "seq", "head"),
        P("seq"),
        P(),
        P(),
    )
    return jax.shard_map(
        on_device, mesh=mesh, in_specs=placed, out_specs=P(("seq", "head"), None), check_vma=False
    )
```

profile of v0, /device:TPU:1, one launch (start us, length us, event | category | flops | bytes accessed | tf_op | source)
XLA Modules:
  0.0 298.3 jit_solution(11702035966844528671)
XLA Ops:
  11.2 4.4 %collective-permute-start = (s32[256]{0:T(256)}, s32[256]{0:T(256)S(1)}, u32[]{:S(2)}, u32[]{:S(2)}) collective-permute-start(s32[256]{0:T(256)} %param.21), channel_id=1, source_target_pairs={{0,8},{8,16},{16,24},{24,32},{32,40},{40,48},{48,56},{56,64},{64,7... | collective-permute-start | bytes 3080 | tf_op jit(solution)/shard_map/ppermute | solution.py:15
  15.6 3.6 %collective-permute-start.2 = (bf16[2,256,128]{2,1,0:T(8,128)(2,1)}, bf16[2,256,128]{2,1,0:T(8,128)(2,1)S(1)}, u32[]{:S(2)}, u32[]{:S(2)}) collective-permute-start(bf16[2,256,128]{2,1,0:T(8,128)(2,1)} %param.20), channel_id=1, source_target_pairs={{0,8},{8,16},{16,24},{24,32},{32,40},{40,48},{48,56},{56,64},{64,7... | collective-permute-start | bytes 393224 | tf_op jit(solution)/shard_map/ppermute | solution.py:15
  22.4 3.1 %multiply_cosine_fusion = (f32[1024,64]{1,0:T(8,128)}, f32[1024,64]{1,0:T(8,128)}) fusion(f32[64]{0:T(128)S(1)} %multiply_exponential_fusion, f32[1024]{0:T(1024)S(1)} %get-tuple-element.196), kind=kLoop, calls=%fused_computation.63 | loop fusion | flops 65536 | bytes 528640 | tf_op jit(solution)/shard_map/cos | solution.py:22
  28.1 30.1 %all-gather.3.cloned.1.call-done = bf16[1024,3072]{1,0:T(8,128)(2,1)} async-done(((bf16[128,3072]{1,0:T(8,128)(2,1)}), bf16[1024,3072]{1,0:T(8,128)(2,1)}) %all-gather.3.cloned.1.call-update) | async-done | bytes 6291472 | tf_op jit(solution)/shard_map/all_gather | solution.py:116
  58.3 5.3 %convolution_bitcast_fusion = f32[1024,1,128]{0,2,1:T(8,128)S(1)} fusion(bf16[1024,3072]{1,0:T(8,128)(2,1)} %all-gather.3.cloned.1.call-done, bf16[3072,128]{1,0:T(8,128)(2,1)} %param.16), kind=kOutput, calls=%fused_computation.51 | convolution fusion | flops 805306368 | bytes 7602176 | tf_op jit(solution)/shard_map/dot_general | solution.py:120
  67.9 4.0 %collective-permute-start.1 = (bf16[2,1024,128]{1,2,0:T(8,128)(2,1)}, bf16[2,1024,128]{1,2,0:T(8,128)(2,1)}, u32[]{:S(2)}, u32[]{:S(2)}) collective-permute-start(bf16[2,1024,128]{1,2,0:T(8,128)(2,1)} %pad_maximum_fusion.1), channel_id=1, source_target_pairs={{0,8},{8,16},{16,24},{24,32},{32,40},{40,48},{48,56},{56,64},{64,7... | collective-permute-start | bytes 1572872 | tf_op jit(solution)/shard_map/ppermute | solution.py:15
  71.9 2.7 fusion.76
  75.6 2.8 copy.74
  84.9 4.6 %collective-permute-done.1 = bf16[2,1024,128]{1,2,0:T(8,128)(2,1)} collective-permute-done((bf16[2,1024,128]{1,2,0:T(8,128)(2,1)}, bf16[2,1024,128]{1,2,0:T(8,128)(2,1)}, u32[]{:S(2)}, u32[]{:S(2)}) %collective-permute-start.1) | collective-permute-done | bytes 524320 | tf_op jit(solution)/shard_map/ppermute | solution.py:15
  91.7 73.2 %while.14 = (s32[]{:T(128)}, f32[2,512,1,3]{1,0,3,2:T(2,128)}, f32[2,512,1,3]{1,0,2,3:T(2,128)}, f32[2,512,1,3,128]{4,1,0,3,2:T(8,128)}, s32[2]{0:T(128)S(1)}, /...) while((s32[]{:T(128)}, f32[2,512,1,3]{1,0,3,2:T(2,128)}, ...), condition=%wide.region_9.10_spmd, body=%wide.region_6.9_spmd.sunk | while | flops 1650459648 | bytes 50030996 | solution.py:179
  100.2 8.1 %fusion.90 = (f32[512,3]{0,1:T(4,128)S(1)}, f32[2048,512,3]{1,0,2:T(8,128)}) fusion(pred[512,2048]{0,1:T(8,128)(4,1)S(1)} %compare_and_fusion.2, bf16[2,512,1,3,128]{4,1,0,3,2:T(8,128)(2,1)} %get-tuple-element.368, s32[]{:T(128)S(6)} %copy.97, bf16[512,1,128]{2,0,1:T(8,128)(2,1)} %get-tuple-element.367, bf16[1536,1,128]{2,0,1:T(8,128)(2,1)} %copy.86), kind=kOutput, calls=%fused_computation.4.clone.1 | convolution fusion | flops 815790592 | bytes 14555140 | tf_op jit(solution)/shard_map/while/body/eval_jaxpr/bgph,ngh->bgpn/dot_general | solution.py:60
  108.4 7.3 %fusion.91 = f32[512,3]{0,1:T(4,128)S(1)} fusion(f32[2048,512,3]{1,0,2:T(8,128)} %get-tuple-element.311, f32[512,3]{0,1:T(4,128)S(1)} %get-tuple-element.310, pred[512,2048]{0,1:T(8,128)(4,1)S(1)} %compare_and_fusion.2), kind=kLoop, calls=%fused_computation.3.clone.1 | loop fusion | flops 12581376 | bytes 13643776 | tf_op jit(solution)/shard_map/while/body/eval_jaxpr/reduce_sum | solution.py:68
  115.8 10.4 %fusion.92 = f32[1,512,1,3,128]{1,4,3,2,0:T(8,128)} fusion(f32[2048,512,3]{1,0,2:T(8,128)} %get-tuple-element.311, f32[512,3]{0,1:T(4,128)S(1)} %get-tuple-element.310, pred[512,2048]{0,1:T(8,128)(4,1)S(1)} %compare_and_fusion.2, bf16[512,1,128]{0,2,1:T(8,128)(2,1)} %get-tuple-element.370, bf16[1536,1,128]{0,2,1:T(8,128)(2,1)} %get-tuple-element.312), kind=kOutput, calls=%fused_computation.9.clone.1 | convolution fusion | flops 818937856 | bytes 14948352 | tf_op jit(solution)/shard_map/while/body/eval_jaxpr/bgpn,ngh->bgph/dot_general | solution.py:69
  137.0 8.1 %fusion.90 = (f32[512,3]{0,1:T(4,128)S(1)}, f32[2048,512,3]{1,0,2:T(8,128)}) fusion(pred[512,2048]{0,1:T(8,128)(4,1)S(1)} %compare_and_fusion.2, bf16[2,512,1,3,128]{4,1,0,3,2:T(8,128)(2,1)} %get-tuple-element.368, s32[]{:T(128)S(6)} %copy.97, bf16[512,1,128]{2,0,1:T(8,128)(2,1)} %get-tuple-element.367, bf16[1536,1,128]{2,0,1:T(8,128)(2,1)} %copy.86), kind=kOutput, calls=%fused_computation.4.clone.1 | convolution fusion | flops 815790592 | bytes 14555140 | tf_op jit(solution)/shard_map/while/body/eval_jaxpr/bgph,ngh->bgpn/dot_general | solution.py:60
  145.2 7.6 %fusion.91 = f32[512,3]{0,1:T(4,128)S(1)} fusion(f32[2048,512,3]{1,0,2:T(8,128)} %get-tuple-element.311, f32[512,3]{0,1:T(4,128)S(1)} %get-tuple-element.310, pred[512,2048]{0,1:T(8,128)(4,1)S(1)} %compare_and_fusion.2), kind=kLoop, calls=%fused_computation.3.clone.1 | loop fusion | flops 12581376 | bytes 13643776 | tf_op jit(solution)/shard_map/while/body/eval_jaxpr/reduce_sum | solution.py:68
  152.9 9.6 %fusion.92 = f32[1,512,1,3,128]{1,4,3,2,0:T(8,128)} fusion(f32[2048,512,3]{1,0,2:T(8,128)} %get-tuple-element.311, f32[512,3]{0,1:T(4,128)S(1)} %get-tuple-element.310, pred[512,2048]{0,1:T(8,128)(4,1)S(1)} %compare_and_fusion.2, bf16[512,1,128]{0,2,1:T(8,128)(2,1)} %get-tuple-element.370, bf16[1536,1,128]{0,2,1:T(8,128)(2,1)} %get-tuple-element.312), kind=kOutput, calls=%fused_computation.9.clone.1 | convolution fusion | flops 818937856 | bytes 14948352 | tf_op jit(solution)/shard_map/while/body/eval_jaxpr/bgpn,ngh->bgph/dot_general | solution.py:69
  164.9 2.7 slice.77
  167.6 3.1 %copy.54 = f32[960,1,3,128]{0,3,2,1:T(8,128)} copy(f32[960,1,3,128]{3,0,2,1:T(8,128)} %slice.77) | data formatting | bytes 2949120 | tf_op jit(solution)/shard_map/slice | solution.py:210
  170.8 33.9 %all-gather.5.cloned.1.call-done = bf16[2,32768,128]{2,1,0:T(8,128)(2,1)} async-done(((bf16[2,1024,128]{2,1,0:T(8,128)(2,1)}), bf16[2,32768,128]{2,1,0:T(8,128)(2,1)}) %all-gather.5.cloned.1.call-update) | async-done | bytes 16777232 | tf_op jit(solution)/shard_map/all_gather | solution.py:197
  204.8 12.3 %fusion.75 = (f32[64,3]{0,1:T(4,128)S(1)}, f32[64,1,3,32768]{3,0,2,1:T(8,128)}) fusion(bf16[2,32768,128]{2,1,0:T(8,128)(2,1)} %all-gather.5.cloned.1.call-done, bf16[1024,3,64]{2,0,1:T(8,128)(2,1)} %copy-done.4, bf16[1024,3,64]{2,0,1:T(8,128)(2,1)S(1)} %copy-done.3), kind=kOutput, calls=%fused_computation.124 | convolution fusion | flops 1623293696 | bytes 34734848 | tf_op jit(solution)/shard_map/bgph,ngh->bgpn/dot_general | solution.py:60
  217.0 10.6 %fusion.23 = f32[64,3]{0,1:T(4,128)S(1)} fusion(f32[64,1,3,32768]{3,0,2,1:T(8,128)} %get-tuple-element.201, f32[64,3]{0,1:T(4,128)S(1)} %get-tuple-element.200), kind=kLoop, calls=%fused_computation.34 | loop fusion | flops 12582720 | bytes 25167360 | tf_op jit(solution)/shard_map/reduce_sum | solution.py:68
  227.7 14.4 %fusion.49 = f32[64,1,3,128]{3,0,2,1:T(8,128)S(1)} fusion(bf16[2,32768,128]{2,1,0:T(8,128)(2,1)} %all-gather.5.cloned.1.call-done, f32[64,1,3,32768]{3,0,2,1:T(8,128)} %get-tuple-element.201, f32[64,3]{0,1:T(4,128)S(1)} %get-tuple-element.200, f32[1024,1,3,128]{3,0,2,1:T(8,128)} %bitcast.189, f32[64,3]{0,1:T(4,128)S(1)} %bitcast.196, ...), kind=kOutput, calls=%fused_computation.59 | convolution fusion | flops 1623318528 | bytes 33754880 | tf_op jit(solution)/shard_map/bgpn,ngh->bgph/dot_general | solution.py:69
  244.3 5.4 %convolution_convert_fusion = bf16[1024,3072]{1,0:T(8,128)(2,1)} fusion(bf16[1024,384]{0,1:T(8,128)(2,1)S(1)} %fusion.32, bf16[384,3072]{1,0:T(8,128)(2,1)S(1)} %copy-done), kind=kOutput, calls=%fused_computation.41 | convolution fusion | flops 2419064832 | bytes 9437184 | tf_op jit(solution)/shard_map/dot_general | solution.py:213
  249.7 42.1 %reduce-scatter.2.cloned.1.call-done = bf16[128,3072]{1,0:T(8,128)(2,1)} async-done(((bf16[1024,3072]{1,0:T(8,128)(2,1)}), bf16[128,3072]{1,0:T(8,128)(2,1)}) %reduce-scatter.2.cloned.1.call-update) | async-done | bytes 786448 | tf_op jit(solution)/shard_map/reduce_scatter | solution.py:212
  (126 shorter events, 47.4 us)
Async XLA Ops:
  6.5 237.7 %copy-start = (bf16[384,3072]{1,0:T(8,128)(2,1)S(1)}, bf16[384,3072]{1,0:T(8,128)(2,1)}, u32[]{:S(2)}) copy-start(bf16[384,3072]{1,0:T(8,128)(2,1)} %param.18) | copy-start | bytes 7077892
  6.5 20.1 %copy-start.8 = (bf16[2,256,128]{2,1,0:T(8,128)(2,1)S(1)}, bf16[2,256,128]{2,1,0:T(8,128)(2,1)}, u32[]{:S(2)}) copy-start(bf16[2,256,128]{2,1,0:T(8,128)(2,1)} %param.20) | copy-start | bytes 393220
  6.5 51.7 %all-gather.3.cloned.1.call-start = ((), (), s32[]{:S(2)}) async-start(), calls=%async_computation.1 | async-start | bytes 7077888 | tf_op jit(solution)/shard_map/all_gather | solution.py:116
  10.4 194.4 %all-gather.5.cloned.1.call-start = ((), (), s32[]{:S(2)}) async-start(), calls=%async_computation.2 | async-start | bytes 17301504 | tf_op jit(solution)/shard_map/all_gather | solution.py:197
  11.1 280.7 %reduce-scatter.2.cloned.1.call-start = ((), (), s32[]{:S(2)}) async-start(), calls=%async_computation.3 | async-start | bytes 7077888 | tf_op jit(solution)/shard_map/reduce_scatter | solution.py:212
  11.2 14.8 %collective-permute-start = (s32[256]{0:T(256)}, s32[256]{0:T(256)S(1)}, u32[]{:S(2)}, u32[]{:S(2)}) collective-permute-start(s32[256]{0:T(256)} %param.21), channel_id=1, source_target_pairs={{0,8},{8,16},{16,24},{24,32},{32,40},{40,48},{48,56},{56,64},{64,7... | collective-permute-start | bytes 3080 | tf_op jit(solution)/shard_map/ppermute | solution.py:15
  15.6 11.1 %collective-permute-start.2 = (bf16[2,256,128]{2,1,0:T(8,128)(2,1)}, bf16[2,256,128]{2,1,0:T(8,128)(2,1)S(1)}, u32[]{:S(2)}, u32[]{:S(2)}) collective-permute-start(bf16[2,256,128]{2,1,0:T(8,128)(2,1)} %param.20), channel_id=1, source_target_pairs={{0,8},{8,16},{16,24},{24,32},{32,40},{40,48},{48,56},{56,64},{64,7... | collective-permute-start | bytes 393224 | tf_op jit(solution)/shard_map/ppermute | solution.py:15
  28.1 36.6 %copy-start.7 = (bf16[3072,128]{1,0:T(8,128)(2,1)S(1)}, bf16[3072,128]{1,0:T(8,128)(2,1)}, u32[]{:S(2)}) copy-start(bf16[3072,128]{1,0:T(8,128)(2,1)} %param.17) | copy-start | bytes 2359300
  58.3 6.5 %copy-start.1 = (bf16[1024,3072]{1,0:T(8,128)(2,1)S(1)}, bf16[1024,3072]{1,0:T(8,128)(2,1)}, u32[]{:S(2)}) copy-start(bf16[1024,3072]{1,0:T(8,128)(2,1)} %all-gather.3.cloned.1.call-done) | copy-start | bytes 18874372
  64.8 7.1 %copy-start.15 = (bf16[3072,384]{1,0:T(8,128)(2,1)S(1)}, bf16[3072,384]{1,0:T(8,128)(2,1)}, u32[]{:S(2)}) copy-start(bf16[3072,384]{1,0:T(8,128)(2,1)} %param.15) | copy-start | bytes 7077892
  67.9 21.6 %collective-permute-start.1 = (bf16[2,1024,128]{1,2,0:T(8,128)(2,1)}, bf16[2,1024,128]{1,2,0:T(8,128)(2,1)}, u32[]{:S(2)}, u32[]{:S(2)}) collective-permute-start(bf16[2,1024,128]{1,2,0:T(8,128)(2,1)} %pad_maximum_fusion.1), channel_id=1, source_target_pairs={{0,8},{8,16},{16,24},{24,32},{32,40},{40,48},{48,56},{56,64},{64,7... | collective-permute-start | bytes 1572872 | tf_op jit(solution)/shard_map/ppermute | solution.py:15
  80.0 9.5 %copy-start.6 = (bf16[1,1024,64]{1,2,0:T(8,128)(2,1)S(1)}, bf16[1,1024,64]{1,2,0:T(8,128)(2,1)}, u32[]{:S(2)}) copy-start(bf16[1,1024,64]{1,2,0:T(8,128)(2,1)} %copy-done.5) | copy-start | bytes 393220
  82.6 2.2 copy-start.4
  100.2 8.1 %copy-start.9 = (f32[2,512,1,3]{1,0,3,2:T(2,128)S(1)}, f32[2,512,1,3]{1,0,3,2:T(2,128)}, u32[]{:S(2)}) copy-start(f32[2,512,1,3]{1,0,3,2:T(2,128)} %get-tuple-element.335) | copy-start | bytes 36868 | tf_op jit(solution)/shard_map/while
  108.4 7.3 %copy-start.10 = (f32[2,512,1,3]{1,0,3,2:T(2,128)}, f32[2,512,1,3]{1,0,3,2:T(2,128)S(1)}, u32[]{:S(2)}) copy-start(f32[2,512,1,3]{1,0,3,2:T(2,128)S(1)} %dynamic_update_slice.16) | copy-start | bytes 36868 | tf_op jit(solution)/shard_map/while
  108.4 7.3 %copy-start.12 = (f32[2,512,1,3]{1,0,2,3:T(2,128)S(1)}, f32[2,512,1,3]{1,0,2,3:T(2,128)}, u32[]{:S(2)}) copy-start(f32[2,512,1,3]{1,0,2,3:T(2,128)} %get-tuple-element.336) | copy-start | bytes 36868 | tf_op jit(solution)/shard_map/while
  115.8 10.4 %copy-start.13 = (f32[2,512,1,3]{1,0,2,3:T(2,128)}, f32[2,512,1,3]{1,0,2,3:T(2,128)S(1)}, u32[]{:S(2)}) copy-start(f32[2,512,1,3]{1,0,2,3:T(2,128)S(1)} %dynamic_update_slice.17) | copy-start | bytes 36868 | tf_op jit(solution)/shard_map/while
  137.0 8.1 %copy-start.9 = (f32[2,512,1,3]{1,0,3,2:T(2,128)S(1)}, f32[2,512,1,3]{1,0,3,2:T(2,128)}, u32[]{:S(2)}) copy-start(f32[2,512,1,3]{1,0,3,2:T(2,128)} %get-tuple-element.335) | copy-start | bytes 36868 | tf_op jit(solution)/shard_map/while
  145.2 7.6 %copy-start.10 = (f32[2,512,1,3]{1,0,3,2:T(2,128)}, f32[2,512,1,3]{1,0,3,2:T(2,128)S(1)}, u32[]{:S(2)}) copy-start(f32[2,512,1,3]{1,0,3,2:T(2,128)S(1)} %dynamic_update_slice.16) | copy-start | bytes 36868 | tf_op jit(solution)/shard_map/while
  145.2 7.6 %copy-start.12 = (f32[2,512,1,3]{1,0,2,3:T(2,128)S(1)}, f32[2,512,1,3]{1,0,2,3:T(2,128)}, u32[]{:S(2)}) copy-start(f32[2,512,1,3]{1,0,2,3:T(2,128)} %get-tuple-element.336) | copy-start | bytes 36868 | tf_op jit(solution)/shard_map/while
  152.9 9.6 %copy-start.13 = (f32[2,512,1,3]{1,0,2,3:T(2,128)}, f32[2,512,1,3]{1,0,2,3:T(2,128)S(1)}, u32[]{:S(2)}) copy-start(f32[2,512,1,3]{1,0,2,3:T(2,128)S(1)} %dynamic_update_slice.17) | copy-start | bytes 36868 | tf_op jit(solution)/shard_map/while
  164.9 5.8 %copy-start.14 = (f32[2,512,1,3]{1,0,2,3:T(2,128)S(1)}, f32[2,512,1,3]{1,0,2,3:T(2,128)}, u32[]{:S(2)}) copy-start(f32[2,512,1,3]{1,0,2,3:T(2,128)} %get-tuple-element.91) | copy-start | bytes 36868
  164.9 5.8 %copy-start.11 = (f32[2,512,1,3]{1,0,3,2:T(2,128)S(1)}, f32[2,512,1,3]{1,0,3,2:T(2,128)}, u32[]{:S(2)}) copy-start(f32[2,512,1,3]{1,0,3,2:T(2,128)} %get-tuple-element.90) | copy-start | bytes 36868
  164.9 39.9 %copy-start.3 = (bf16[1024,3,64]{2,0,1:T(8,128)(2,1)S(1)}, bf16[1024,3,64]{2,0,1:T(8,128)(2,1)}, u32[]{:S(2)}) copy-start(bf16[1024,3,64]{2,0,1:T(8,128)(2,1)} %copy-done.2) | copy-start | bytes 1179652
  (2 other events, 3.2 us)
Sparse Core Ops, SparseCore 0:
  10.5 47.6 all-gather.2
  60.8 143.8 all-gather.4
  249.8 41.9 reduce-scatter.1
where the time goes:
time: 299 us; the launch traced here: 298 us
  waiting for transfers between devices  111 us (37%)
  matrix products  78.4 us (26%)
  other arithmetic  49.5 us (17%)
  local copies, waits for them, and re-layouts  31.9 us (11%)
  between operations  13.4 us (4%)
  starting transfers between devices  12 us (4%)
    reduce_scatter x1, waiting for transfers between devices, on_device(): lax.psum_scatter(jnp.dot(attended, w_out, preferred_element_type=jnp.floa...  42.1 us
    dot_general x3, matrix products, finish_state(): jnp.einsum('bgpn,ngh->bgph', weights.astype(jnp.bfloat16), values, prefer...  34.4 us
    all_gather x1, waiting for transfers between devices, on_device(): piece = lax.all_gather(long_cache, 'seq', axis=1, tiled=True)  33.9 us
    all_gather x1, waiting for transfers between devices, on_device(): piece = lax.all_gather(normed, 'head', axis=0, tiled=True)  30.1 us
    dot_general x3, matrix products, raw_scores(): jnp.einsum('bgph,ngh->bgpn', queries, keys, preferred_element_type=jnp.fl...  28.4 us
    reduce_sum x3, other arithmetic, finish_state(): summed = jnp.sum(weights, axis=-1)  25.5 us
    ppermute x3, starting transfers between devices, from_behind(): return lax.ppermute(block, axis, route)  11.9 us
  transfers between devices with their start and end apart: 6, of which 4 were waited for; matrix products, arithmetic and copies ran while one was open for 37% of the time, Pallas kernels for 0%

commit v1 on v0

--- a/solution.py
+++ b/solution.py
@@ -194,7 +194,9 @@
         jnp.zeros((LEAD, kv_heads, per_kv), jnp.float32),
         jnp.zeros((LEAD, kv_heads, per_kv, HD), jnp.float32),
     )
-    piece = lax.all_gather(long_cache, "seq", axis=1, tiled=True)
+    piece = jnp.concatenate(
+        lax.all_to_all(jnp.stack([long_cache] * lax.axis_size("seq")), "seq", 0, 0), axis=1
+    )
     long_state = combine(
         start_state,
         plain_state(

time: 299 us -> 655 us (2.19)
  waiting for transfers between devices: 111 us -> 438 us
  local copies, waits for them, and re-layouts: 31.9 us -> 51 us
  starting transfers between devices: 12 us -> 23.3 us
    ppermute x3, waiting for transfers between devices: 4.59 us -> 378 us  [from_behind(): return lax.ppermute(block, axis, route)]
    all_gather x1 -> x0, waiting for transfers between devices: 33.9 us -> none  [on_device(): piece = lax.all_gather(long_cache, 'seq', axis=1, tiled=True)]
    all_gather x1, waiting for transfers between devices: 30.1 us -> 0.01 us  [on_device(): piece = lax.all_gather(normed, 'head', axis=0, tiled=True)]
    reduce_scatter x1, waiting for transfers between devices: 42.1 us -> 59.8 us  [on_device(): lax.psum_scatter(jnp.dot(attended, w_out, preferred_element_type=jnp.floa...]
    all_to_all x0 -> x1, starting transfers between devices: none -> 12.1 us  [on_device(): lax.all_to_all(jnp.stack([long_cache] * lax.axis_size('seq')), 'seq', 0, 0)]
    slice x0 -> x1, local copies, waits for them, and re-layouts: none -> 11.9 us  [on_device(): piece[0].reshape(-1, kv_heads, HD)]
  transfers between devices with their start and end apart: 6 -> 6, of which waited for: 4 -> 3; matrix products, arithmetic and copies ran while one was open for 37% -> 17% of each run, Pallas kernels for 0% -> 0%
where the time goes in v1:
time: 655 us; the launch traced here: 654 us
  waiting for transfers between devices  438 us (67%)
  matrix products  79.9 us (12%)
  local copies, waits for them, and re-layouts  51 us (8%)
  other arithmetic  46.3 us (7%)
  starting transfers between devices  23.3 us (4%)
  between operations  13.8 us (2%)
    ppermute x3, waiting for transfers between devices, from_behind(): return lax.ppermute(block, axis, route)  378 us
    reduce_scatter x1, waiting for transfers between devices, on_device(): lax.psum_scatter(jnp.dot(attended, w_out, preferred_element_type=jnp.floa...  59.8 us
    dot_general x3, matrix products, finish_state(): jnp.einsum('bgpn,ngh->bgph', weights.astype(jnp.bfloat16), values, prefer...  33 us
    dot_general x3, matrix products, raw_scores(): jnp.einsum('bgph,ngh->bgpn', queries, keys, preferred_element_type=jnp.fl...  31.1 us
    reduce_sum x3, other arithmetic, finish_state(): summed = jnp.sum(weights, axis=-1)  25.2 us
  transfers between devices with their start and end apart: 6, of which 3 were waited for; matrix products, arithmetic and copies ran while one was open for 17% of the time, Pallas kernels for 0%

profile of v1, /device:TPU:1, one launch (start us, length us, event | category | flops | bytes accessed | tf_op | source)
XLA Modules:
  0.0 653.9 jit_solution(5804633739221457527)
XLA Ops:
  6.5 7.1 %stack.8 = bf16[32,2,1024,128]{3,2,1,0:T(8,128)(2,1)} broadcast(bf16[2,1024,128]{2,1,0:T(8,128)(2,1)} %param.19), dimensions={1,2,3} | broadcast | bytes 17301504 | tf_op jit(solution)/shard_map/stack | solution.py:198
  13.7 12.1 %all-to-all-start = ((bf16[32,2,1024,128]{3,2,1,0:T(8,128)(2,1)}), bf16[32,2,1024,128]{3,2,1,0:T(8,128)(2,1)}, u32[]{:S(2)}, u32[]{:S(2)}) async-start(bf16[32,2,1024,128]{3,2,1,0:T(8,128)(2,1)} %stack.8), calls=%async_computation | async-start | bytes 33554432 | tf_op jit(solution)/shard_map/all_to_all | solution.py:198
  27.4 3.1 collective-permute-start
  30.5 3.1 collective-permute-start.2
  34.9 3.0 multiply_cosine_fusion
  38.5 376.0 %collective-permute-done = s32[256]{0:T(256)S(1)} collective-permute-done((s32[256]{0:T(256)}, s32[256]{0:T(256)S(1)}, u32[]{:S(2)}, u32[]{:S(2)}) %collective-permute-start) | collective-permute-done | bytes 1056 | tf_op jit(solution)/shard_map/ppermute | solution.py:15
  418.9 5.3 convolution_bitcast_fusion
  429.3 4.9 collective-permute-start.1
  434.2 2.7 fusion.77
  438.0 2.7 copy.90
  449.3 71.0 %while.14 = (s32[]{:T(128)}, f32[2,512,1,3]{1,0,3,2:T(2,128)}, f32[2,512,1,3]{1,0,2,3:T(2,128)}, f32[2,512,1,3,128]{4,1,0,3,2:T(8,128)}, s32[2]{0:T(128)S(1)}, /...) while((s32[]{:T(128)}, f32[2,512,1,3]{1,0,3,2:T(2,128)}, ...), condition=%wide.region_9.10_spmd, body=%wide.region_6.9_spmd.sunk | while | flops 1650459648 | bytes 50030996 | solution.py:179
  457.6 8.0 %fusion.93 = (f32[512,3]{0,1:T(4,128)S(1)}, f32[2048,512,3]{1,0,2:T(8,128)}) fusion(pred[512,2048]{0,1:T(8,128)(4,1)S(1)} %compare_and_fusion.2, bf16[2,512,1,3,128]{4,1,0,3,2:T(8,128)(2,1)} %get-tuple-element.386, s32[]{:T(128)S(6)} %copy.113, bf16[512,1,128]{2,0,1:T(8,128)(2,1)} %get-tuple-element.385, bf16[1536,1,128]{2,0,1:T(8,128)(2,1)} %copy.102), kind=kOutput, calls=%fused_computation.4.clone.1 | convolution fusion | flops 815790592 | bytes 14555140 | tf_op jit(solution)/shard_map/while/body/eval_jaxpr/bgph,ngh->bgpn/dot_general | solution.py:60
  465.7 7.3 %fusion.94 = f32[512,3]{0,1:T(4,128)S(1)} fusion(f32[2048,512,3]{1,0,2:T(8,128)} %get-tuple-element.329, f32[512,3]{0,1:T(4,128)S(1)} %get-tuple-element.328, pred[512,2048]{0,1:T(8,128)(4,1)S(1)} %compare_and_fusion.2), kind=kLoop, calls=%fused_computation.3.clone.1 | loop fusion | flops 12581376 | bytes 13643776 | tf_op jit(solution)/shard_map/while/body/eval_jaxpr/reduce_sum | solution.py:68
  473.1 9.3 %fusion.95 = f32[1,512,1,3,128]{1,4,3,2,0:T(8,128)} fusion(f32[2048,512,3]{1,0,2:T(8,128)} %get-tuple-element.329, f32[512,3]{0,1:T(4,128)S(1)} %get-tuple-element.328, pred[512,2048]{0,1:T(8,128)(4,1)S(1)} %compare_and_fusion.2, bf16[512,1,128]{0,2,1:T(8,128)(2,1)} %get-tuple-element.388, bf16[1536,1,128]{0,2,1:T(8,128)(2,1)} %get-tuple-element.330), kind=kOutput, calls=%fused_computation.9.clone.1 | convolution fusion | flops 818937856 | bytes 14948352 | tf_op jit(solution)/shard_map/while/body/eval_jaxpr/bgpn,ngh->bgph/dot_general | solution.py:69
  493.1 8.0 %fusion.93 = (f32[512,3]{0,1:T(4,128)S(1)}, f32[2048,512,3]{1,0,2:T(8,128)}) fusion(pred[512,2048]{0,1:T(8,128)(4,1)S(1)} %compare_and_fusion.2, bf16[2,512,1,3,128]{4,1,0,3,2:T(8,128)(2,1)} %get-tuple-element.386, s32[]{:T(128)S(6)} %copy.113, bf16[512,1,128]{2,0,1:T(8,128)(2,1)} %get-tuple-element.385, bf16[1536,1,128]{2,0,1:T(8,128)(2,1)} %copy.102), kind=kOutput, calls=%fused_computation.4.clone.1 | convolution fusion | flops 815790592 | bytes 14555140 | tf_op jit(solution)/shard_map/while/body/eval_jaxpr/bgph,ngh->bgpn/dot_general | solution.py:60
  501.2 7.3 %fusion.94 = f32[512,3]{0,1:T(4,128)S(1)} fusion(f32[2048,512,3]{1,0,2:T(8,128)} %get-tuple-element.329, f32[512,3]{0,1:T(4,128)S(1)} %get-tuple-element.328, pred[512,2048]{0,1:T(8,128)(4,1)S(1)} %compare_and_fusion.2), kind=kLoop, calls=%fused_computation.3.clone.1 | loop fusion | flops 12581376 | bytes 13643776 | tf_op jit(solution)/shard_map/while/body/eval_jaxpr/reduce_sum | solution.py:68
  508.6 9.3 %fusion.95 = f32[1,512,1,3,128]{1,4,3,2,0:T(8,128)} fusion(f32[2048,512,3]{1,0,2:T(8,128)} %get-tuple-element.329, f32[512,3]{0,1:T(4,128)S(1)} %get-tuple-element.328, pred[512,2048]{0,1:T(8,128)(4,1)S(1)} %compare_and_fusion.2, bf16[512,1,128]{0,2,1:T(8,128)(2,1)} %get-tuple-element.388, bf16[1536,1,128]{0,2,1:T(8,128)(2,1)} %get-tuple-element.330), kind=kOutput, calls=%fused_computation.9.clone.1 | convolution fusion | flops 818937856 | bytes 14948352 | tf_op jit(solution)/shard_map/while/body/eval_jaxpr/bgpn,ngh->bgph/dot_general | solution.py:69
  522.9 3.0 copy.70
  527.5 11.9 %fusion.74 = (bf16[1,32,1024,128]{3,2,0,1:T(8,128)(2,1)}, bf16[1,32,1024,128]{3,2,0,1:T(8,128)(2,1)}) fusion(bf16[2,32,1024,128]{3,2,0,1:T(8,128)(2,1)} %bitcast.28), kind=kLoop, calls=%fused_computation.121 | loop fusion | bytes 33554432 | tf_op jit(solution)/shard_map/slice | solution.py:203
  539.3 15.2 %fusion.76 = (f32[64,3]{0,1:T(4,128)S(1)}, f32[64,1,3,32768]{3,0,2,1:T(8,128)}) fusion(bf16[32768,128,1]{1,0,2:T(8,128)(2,1)} %bitcast.173, bf16[1024,3,64]{2,0,1:T(8,128)(2,1)S(1)} %copy-done.5, bf16[1024,3,64]{2,0,1:T(8,128)(2,1)S(1)} %copy-done.3), kind=kOutput, calls=%fused_computation.123 | convolution fusion | flops 1623293696 | bytes 34341632 | tf_op jit(solution)/shard_map/bgph,ngh->bgpn/dot_general | solution.py:60
  554.5 10.6 %fusion.23 = f32[64,3]{0,1:T(4,128)S(1)} fusion(f32[64,1,3,32768]{3,0,2,1:T(8,128)} %get-tuple-element.219, f32[64,3]{0,1:T(4,128)S(1)} %get-tuple-element.218), kind=kLoop, calls=%fused_computation.34 | loop fusion | flops 12582720 | bytes 25167360 | tf_op jit(solution)/shard_map/reduce_sum | solution.py:68
  565.2 14.4 %fusion.49 = f32[64,1,3,128]{3,0,2,1:T(8,128)S(1)} fusion(bf16[32768,128,1]{1,0,2:T(8,128)(2,1)} %bitcast.172, f32[64,1,3,32768]{3,0,2,1:T(8,128)} %get-tuple-element.219, f32[64,3]{0,1:T(4,128)S(1)} %get-tuple-element.218, f32[1024,1,3,128]{3,0,2,1:T(8,128)} %bitcast.178, f32[64,3]{0,1:T(4,128)S(1)} %bitcast.185, f32[64,3]{0,1:T(4,128)S(1)} %get-tuple-element.217, ...), kind=kOutput, calls=%fused_computation.57 | convolution fusion | flops 1623318528 | bytes 33754880 | tf_op jit(solution)/shard_map/bgpn,ngh->bgph/dot_general | solution.py:69
  581.7 5.5 convolution_convert_fusion
  587.2 59.8 %reduce-scatter.2.cloned.1.call-done = bf16[128,3072]{1,0:T(8,128)(2,1)} async-done(((bf16[1024,3072]{1,0:T(8,128)(2,1)}), bf16[128,3072]{1,0:T(8,128)(2,1)}) %reduce-scatter.2.cloned.1.call-update) | async-done | bytes 786448 | tf_op jit(solution)/shard_map/reduce_scatter | solution.py:214
  (137 shorter events, 48.9 us)
Async XLA Ops:
  6.5 575.2 %copy-start = (bf16[384,3072]{1,0:T(8,128)(2,1)S(1)}, bf16[384,3072]{1,0:T(8,128)(2,1)}, u32[]{:S(2)}) copy-start(bf16[384,3072]{1,0:T(8,128)(2,1)} %param.18) | copy-start | bytes 7077892
  13.7 12.2 %copy-start.6 = (bf16[128,3072]{1,0:T(8,128)(2,1)S(1)}, bf16[128,3072]{1,0:T(8,128)(2,1)}, u32[]{:S(2)}) copy-start(bf16[128,3072]{1,0:T(8,128)(2,1)} %param.13) | copy-start | bytes 2359300
  13.7 12.5 %copy-start.12 = (f32[3072]{0:T(1024)S(1)}, f32[3072]{0:T(1024)}, u32[]{:S(2)}) copy-start(f32[3072]{0:T(1024)} %param.14) | copy-start | bytes 36868
  13.7 16.8 %copy-start.10 = (bf16[2,256,128]{2,1,0:T(8,128)(2,1)S(1)}, bf16[2,256,128]{2,1,0:T(8,128)(2,1)}, u32[]{:S(2)}) copy-start(bf16[2,256,128]{2,1,0:T(8,128)(2,1)} %param.20) | copy-start | bytes 393220
  13.7 19.9 %copy-start.18 = (s32[64]{0:T(128)S(1)}, s32[64]{0:T(128)}, u32[]{:S(2)}) copy-start(s32[64]{0:T(128)} %param.22) | copy-start | bytes 772
  13.7 20.3 %copy-start.19 = (s32[64]{0:T(128)S(1)}, s32[64]{0:T(128)}, u32[]{:S(2)}) copy-start(s32[64]{0:T(128)} %param.23) | copy-start | bytes 772
  13.7 513.7 %all-to-all-start = ((bf16[32,2,1024,128]{3,2,1,0:T(8,128)(2,1)}), bf16[32,2,1024,128]{3,2,1,0:T(8,128)(2,1)}, u32[]{:S(2)}, u32[]{:S(2)}) async-start(bf16[32,2,1024,128]{3,2,1,0:T(8,128)(2,1)} %stack.8), calls=%async_computation | async-start | bytes 33554432 | tf_op jit(solution)/shard_map/all_to_all | solution.py:198
  25.8 393.0 %all-gather.2.cloned.1.call-start = ((), (), s32[]{:S(2)}) async-start(), calls=%async_computation.2 | async-start | bytes 7077888 | tf_op jit(solution)/shard_map/all_gather | solution.py:116
  27.3 619.7 %reduce-scatter.2.cloned.1.call-start = ((), (), s32[]{:S(2)}) async-start(), calls=%async_computation.3 | async-start | bytes 7077888 | tf_op jit(solution)/shard_map/reduce_scatter | solution.py:214
  27.4 387.1 %collective-permute-start = (s32[256]{0:T(256)}, s32[256]{0:T(256)S(1)}, u32[]{:S(2)}, u32[]{:S(2)}) collective-permute-start(s32[256]{0:T(256)} %param.21), channel_id=1, source_target_pairs={{0,8},{8,16},{16,24},{24,32},{32,40},{40,48},{48,56},{56,64},{64,7... | collective-permute-start | bytes 3080 | tf_op jit(solution)/shard_map/ppermute | solution.py:15
  30.5 386.9 %collective-permute-start.2 = (bf16[2,256,128]{2,1,0:T(8,128)(2,1)S(1)}, bf16[2,256,128]{2,1,0:T(8,128)(2,1)S(1)}, u32[]{:S(2)}, u32[]{:S(2)}) collective-permute-start(bf16[2,256,128]{2,1,0:T(8,128)(2,1)S(1)} %copy-done.10), channel_id=1, source_target_pairs={{0,8},{8,16},{16,24},{24,32},{32,40},{40,48},{48,56},{56,64},{64,7... | collective-permute-start | bytes 393224 | tf_op jit(solution)/shard_map/ppermute | solution.py:15
  34.2 384.6 %copy-start.11 = (f32[1024]{0:T(1024)}, f32[1024]{0:T(1024)S(1)}, u32[]{:S(2)}) copy-start(f32[1024]{0:T(1024)S(1)} %get-tuple-element.214) | copy-start | bytes 12292
  34.3 384.6 %copy-start.17 = (f32[64]{0:T(128)}, f32[64]{0:T(128)S(1)}, u32[]{:S(2)}) copy-start(f32[64]{0:T(128)S(1)} %multiply_exponential_fusion) | copy-start | bytes 772
  417.4 8.8 %copy-start.9 = (bf16[3072,128]{1,0:T(8,128)(2,1)S(1)}, bf16[3072,128]{1,0:T(8,128)(2,1)}, u32[]{:S(2)}) copy-start(bf16[3072,128]{1,0:T(8,128)(2,1)} %param.17) | copy-start | bytes 2359300
  418.9 7.4 %copy-start.1 = (bf16[1024,3072]{1,0:T(8,128)(2,1)S(1)}, bf16[1024,3072]{1,0:T(8,128)(2,1)}, u32[]{:S(2)}) copy-start(bf16[1024,3072]{1,0:T(8,128)(2,1)} %all-gather.2.cloned.1.call-done) | copy-start | bytes 18874372
  424.2 10.0 %copy-start.20 = (bf16[3072,384]{1,0:T(8,128)(2,1)S(1)}, bf16[3072,384]{1,0:T(8,128)(2,1)}, u32[]{:S(2)}) copy-start(bf16[3072,384]{1,0:T(8,128)(2,1)} %param.15) | copy-start | bytes 7077892
  429.3 17.8 %collective-permute-start.1 = (bf16[2,1024,128]{1,2,0:T(8,128)(2,1)}, bf16[2,1024,128]{1,2,0:T(8,128)(2,1)}, u32[]{:S(2)}, u32[]{:S(2)}) collective-permute-start(bf16[2,1024,128]{1,2,0:T(8,128)(2,1)} %pad_maximum_fusion.1), channel_id=1, source_target_pairs={{0,8},{8,16},{16,24},{24,32},{32,40},{40,48},{48,56},{56,64},{64,7... | collective-permute-start | bytes 1572872 | tf_op jit(solution)/shard_map/ppermute | solution.py:15
  457.6 8.0 %copy-start.13 = (f32[2,512,1,3]{1,0,3,2:T(2,128)S(1)}, f32[2,512,1,3]{1,0,3,2:T(2,128)}, u32[]{:S(2)}) copy-start(f32[2,512,1,3]{1,0,3,2:T(2,128)} %get-tuple-element.353) | copy-start | bytes 36868 | tf_op jit(solution)/shard_map/while
  465.7 7.3 %copy-start.15 = (f32[2,512,1,3]{1,0,2,3:T(2,128)S(1)}, f32[2,512,1,3]{1,0,2,3:T(2,128)}, u32[]{:S(2)}) copy-start(f32[2,512,1,3]{1,0,2,3:T(2,128)} %get-tuple-element.354) | copy-start | bytes 36868 | tf_op jit(solution)/shard_map/while
  473.1 9.3 %copy-start.16 = (f32[2,512,1,3]{1,0,2,3:T(2,128)}, f32[2,512,1,3]{1,0,2,3:T(2,128)S(1)}, u32[]{:S(2)}) copy-start(f32[2,512,1,3]{1,0,2,3:T(2,128)S(1)} %dynamic_update_slice.17) | copy-start | bytes 36868 | tf_op jit(solution)/shard_map/while
  493.1 8.0 %copy-start.13 = (f32[2,512,1,3]{1,0,3,2:T(2,128)S(1)}, f32[2,512,1,3]{1,0,3,2:T(2,128)}, u32[]{:S(2)}) copy-start(f32[2,512,1,3]{1,0,3,2:T(2,128)} %get-tuple-element.353) | copy-start | bytes 36868 | tf_op jit(solution)/shard_map/while
  508.6 9.3 %copy-start.16 = (f32[2,512,1,3]{1,0,2,3:T(2,128)}, f32[2,512,1,3]{1,0,2,3:T(2,128)S(1)}, u32[]{:S(2)}) copy-start(f32[2,512,1,3]{1,0,2,3:T(2,128)S(1)} %dynamic_update_slice.17) | copy-start | bytes 36868 | tf_op jit(solution)/shard_map/while
  527.4 11.9 %copy-start.3 = (bf16[1024,3,64]{2,0,1:T(8,128)(2,1)S(1)}, bf16[1024,3,64]{2,0,1:T(8,128)(2,1)}, u32[]{:S(2)}) copy-start(bf16[1024,3,64]{2,0,1:T(8,128)(2,1)} %copy-done.2) | copy-start | bytes 1179652
  527.5 11.9 %copy-start.5 = (bf16[1024,3,64]{2,0,1:T(8,128)(2,1)S(1)}, bf16[1024,3,64]{2,0,1:T(8,128)(2,1)}, u32[]{:S(2)}) copy-start(bf16[1024,3,64]{2,0,1:T(8,128)(2,1)} %copy-done.4) | copy-start | bytes 1179652
  (7 other events, 32.9 us)
Sparse Core Ops, SparseCore 0:
  28.5 45.5 all-gather.1
  587.4 59.6 reduce-scatter.1
